TPU v7x, 512 devices: a whole 4x8x8 slice. The times are simulated.
512 devices in a mesh: layer: 4 (over x), feat: 32 (over z, y_lo), width: 4 (over y_hi, core).
Axes of the slice: x: 4, y: 8 (y_hi: 2, y_lo: 4; y = y_hi * 4 + y_lo), z: 8, core: 2. Of those that a mesh axis runs over, the one named last changes fastest.
Arguments:
- residuals: bfloat16 [4, 1024, 2304], P('layer', 'feat', 'width'), may hold values from -6 to 6
- cotangent: bfloat16 [4, 1024, 2304], P('layer', 'feat', 'width'), may hold values from -6 to 6
- enc_weight: bfloat16 [4, 2304, 8192], P('layer', 'width', 'feat'), may hold values from -0.125 to 0.125
- enc_bias: float32 [4, 8192], P('layer', 'feat'), may hold values from -3 to 3
- dec_weight: bfloat16 [4, 4, 8192, 2304], P('layer', None, 'feat', 'width'), may hold values from -0.0625 to 0.0625
- active: int32 [4, 1024, 8192], P('layer', None, 'feat'), may hold values 0 or 1
Outputs:
- dec_grad: bfloat16 [4, 4, 8192, 2304], P('layer', None, 'feat', 'width')
- enc_grad: bfloat16 [4, 2304, 8192], P('layer', 'width', 'feat')
- bias_grad: float32 [4, 8192], P('layer', 'feat')
- feat_grad: bfloat16 [4, 1024, 8192], P('layer', None, 'feat')
All inputs are finite; a program needn't handle non-finite values. No bound on the sum of `active` on one device may be relied on, other than what follows from the above.
Results may differ from a plain program's by a relative error of at most 0.005.
Values may be sent and summed in bfloat16 or wider, within the bound.
A program may use at most 64 MiB of HBM per device.

v0:
```python
import jax
import jax.numpy as jnp
from jax import lax
from jax.sharding import PartitionSpec as P


def local(residuals, cotangent, enc_weight, enc_bias, dec_weight, active):
    layers = dec_weight.shape[1]
    source = lax.axis_index("layer")
    local_grads = lax.all_gather(cotangent, "layer", axis=0, tiled=True)
    whole_resid, whole_grads = (
        lax.all_gather(residuals[0], "feat", axis=0, tiled=True),
        lax.all_gather(local_grads, "feat", axis=1, tiled=True),
    )
    later_mask = (jnp.arange(layers) >= source)[:, None, None]
    used_grads = jnp.where(later_mask, whole_grads, jnp.zeros_like(whole_grads))
    enc_part = jnp.dot(whole_resid, enc_weight[0], preferred_element_type=jnp.float32)
    feat_part = jnp.einsum(
        "ktd,kfd->tf", used_grads, dec_weight[0], preferred_element_type=jnp.float32
    )
    enc_total, feat_total = lax.psum((enc_part, feat_part), "width")
    gate_all = active[0].astype(jnp.float32)
    activation = ((enc_total + enc_bias) * gate_all).astype(jnp.bfloat16)
    feat_grad = (feat_total * gate_all).astype(jnp.bfloat16)
    dec_grad = jnp.einsum(
        "tf,ktd->kfd", activation, used_grads, preferred_element_type=jnp.float32
    ).astype(jnp.bfloat16)
    enc_grad = lax.dot_general(
        whole_resid, feat_grad, (((0,), (0,)), ((), ())), preferred_element_type=jnp.float32
    ).astype(jnp.bfloat16)
    bias_grad = jnp.sum(feat_grad, axis=0, dtype=jnp.float32)
    return (dec_grad[None], enc_grad[None], bias_grad[None], feat_grad[None])


def solution(mesh):
    in_specs = (
        P("layer", "feat", "width"),
        P("layer", "feat", "width"),
        P("layer", "width", "feat"),
        P("layer", "feat"),
        P("layer", None, "feat", "width"),
        P("layer", None, "feat"),
    )
    out_specs = (
        P("layer", None, "feat", "width"),
        P("layer", "width", "feat"),
        P("layer", "feat"),
        P("layer", None, "feat"),
    )
    return jax.shard_map(local, mesh=mesh, in_specs=in_specs, out_specs=out_specs, check_vma=False)
```

profile of v0, /device:TPU:1, one launch (start us, length us, event | category | flops | bytes accessed | tf_op | source)
XLA Modules:
  0.0 466.8 jit_solution(9379940428828128747)
XLA Ops:
  7.2 0.0 copy-start
  7.2 0.0 all-gather.6.cloned.1.call-start
  7.2 0.7 all-gather.6.cloned.1.call-update
  7.9 0.0 all-gather.4.cloned.1.call-start
  8.0 12.6 %all_gather.9 = bf16[4,32,576]{2,1,0:T(8,128)(2,1)} all-gather(bf16[1,32,576]{2,1,0:T(8,128)(2,1)} %param.7), channel_id=1, replica_groups=mesh['layer'=4,'feat'=32,'width'=4] {'layer'}, dimensions={0}, use_global_device_ids=true | all-gather | bytes 184320 | tf_op jit(solution)/shard_map/all_gather | solution.py:10
  20.5 0.0 all-gather.4.cloned.1.call-update
  20.6 0.0 all-reduce.3.cloned.1.call-start
  20.6 127.4 %all-gather.6.cloned.1.call-done = bf16[1,1024,576]{2,1,0:T(8,128)(2,1)} async-done(((bf16[1,32,576]{2,1,0:T(8,128)(2,1)}), bf16[1,1024,576]{2,1,0:T(8,128)(2,1)}) %all-gather.6.cloned.1.call-update) | async-done | bytes 1179664 | tf_op jit(solution)/shard_map/all_gather | solution.py:12
  148.0 2.9 fusion.7
  150.9 171.4 %all-gather.4.cloned.1.call-done = bf16[4,1024,576]{2,1,0:T(8,128)(2,1)} async-done(((bf16[4,32,576]{2,1,0:T(8,128)(2,1)}), bf16[4,1024,576]{2,1,0:T(8,128)(2,1)}) %all-gather.4.cloned.1.call-update) | async-done | bytes 4718608 | tf_op jit(solution)/shard_map/all_gather | solution.py:13
  322.3 0.0 copy-done
  322.3 5.2 %fusion.4 = f32[1024,256]{1,0:T(8,128)} fusion(bf16[4,1024,576]{2,1,0:T(8,128)(2,1)} %all-gather.4.cloned.1.call-done, pred[4]{0:T(512)(128)(4,1)S(1)} %iota_compare_fusion, bf16[1,4,256,576]{2,3,1,0:T(8,128)(2,1)S(1)} %copy-done), kind=kOutput, calls=%fused_computation.5 | convolution fusion | flops 1210318848 | bytes 6946820 | tf_op jit(solution)/shard_map/ktd,kfd->tf/dot_general | solution.py:18
  327.4 0.0 copy-start.3
  327.4 0.0 copy-start.1
  327.4 0.0 all-reduce.3.cloned.1.call-update
  327.5 124.2 %all-reduce.3.cloned.1.call-done = (f32[1024,256]{1,0:T(8,128)}, f32[1024,256]{1,0:T(8,128)}) async-done(((f32[1024,256]{1,0:T(8,128)}, f32[1024,256]{1,0:T(8,128)}), (f32[1024,256]{1,0:T(8,128)}, f32[1024,256]{1,0:T(8,128)})) %all-reduce.3.cloned.1.call-update) | async-done | bytes 2097168 | tf_op jit(solution)/shard_map/psum | solution.py:21
  451.7 0.0 copy-done.3
  451.7 2.1 convert_reduce_fusion
  453.8 0.0 copy-done.1
  453.8 1.3 fusion.13
  455.1 0.0 copy-done.4
  455.1 0.0 copy-done.5
  455.1 5.2 %fusion.3 = bf16[1,4,256,576]{2,3,1,0:T(8,128)(2,1)} fusion(bf16[4,1024,576]{2,1,0:T(8,128)(2,1)} %all-gather.4.cloned.1.call-done, pred[4]{0:T(512)(128)(4,1)S(1)} %iota_compare_fusion, s32[1,1024,256]{2,1,0:T(8,128)S(1)} %copy-done.3, f32[1024,256]{1,0:T(8,128)S(1)} %copy-done.4, f32[256]{0:T(256)S(1)} %bitcast.45), kind=kOutput, calls=%fused_computation.4 | convolution fusion | flops 1211957248 | bytes 7996420 | tf_op jit(solution)/shard_map/tf,ktd->kfd/dot_general | solution.py:25
  460.3 0.0 copy-done.2
  (4 shorter events, 0.0 us)
Async XLA Ops:
  7.2 315.1 %copy-start = (bf16[1,4,256,576]{2,3,1,0:T(8,128)(2,1)S(1)}, bf16[1,4,256,576]{2,3,1,0:T(8,128)(2,1)}, u32[]{:S(2)}) copy-start(bf16[1,4,256,576]{2,3,1,0:T(8,128)(2,1)} %param.10) | copy-start | bytes 3538948
  7.2 140.8 %all-gather.6.cloned.1.call-start = ((), (), s32[]{:S(2)}) async-start(), calls=%async_computation.1 | async-start | bytes 1351680 | tf_op jit(solution)/shard_map/all_gather | solution.py:12
  7.9 314.4 %all-gather.4.cloned.1.call-start = ((), (), s32[]{:S(2)}) async-start(), calls=%async_computation | async-start | bytes 5406720 | tf_op jit(solution)/shard_map/all_gather | solution.py:13
  20.6 431.1 %all-reduce.3.cloned.1.call-start = ((), (), s32[]{:S(2)}) async-start(), calls=%async_computation.2 | async-start | bytes 4194304 | tf_op jit(solution)/shard_map/psum | solution.py:21
  327.4 124.2 %copy-start.3 = (s32[1,1024,256]{2,1,0:T(8,128)S(1)}, s32[1,1024,256]{2,1,0:T(8,128)}, u32[]{:S(2)}) copy-start(s32[1,1024,256]{2,1,0:T(8,128)} %param.11) | copy-start | bytes 3145732
  327.4 126.3 %copy-start.1 = (bf16[1,1024,576]{2,1,0:T(8,128)(2,1)S(1)}, bf16[1,1024,576]{2,1,0:T(8,128)(2,1)}, u32[]{:S(2)}) copy-start(bf16[1,1024,576]{2,1,0:T(8,128)(2,1)} %all-gather.6.cloned.1.call-done) | copy-start | bytes 3538948
  451.7 3.4 copy-start.4
  451.7 3.4 copy-start.5
  453.8 6.5 %copy-start.2 = (bf16[1024,256]{1,0:T(8,128)(2,1)}, bf16[1024,256]{1,0:T(8,128)(2,1)S(1)}, u32[]{:S(2)}) copy-start(bf16[1024,256]{1,0:T(8,128)(2,1)S(1)} %get-tuple-element.7) | copy-start | bytes 1572868
Sparse Core Ops, SparseCore 0:
  10.1 137.8 all-gather.5
  150.1 172.1 all-gather.3
  327.6 124.0 all-reduce.2
where the time goes:
time: 467 us
  waiting for transfers between devices  424 us (91%)
  matrix products  14.6 us (3%)
  between operations  13.8 us (3%)
  blocking collectives  12.6 us (3%)
    all_gather x1, waiting for transfers between devices, local(): lax.all_gather(local_grads, 'feat', axis=1, tiled=True)  171 us
    all_gather x1, waiting for transfers between devices, local(): lax.all_gather(residuals[0], 'feat', axis=0, tiled=True)  127 us
    psum x1, waiting for transfers between devices, local(): enc_total, feat_total = lax.psum((enc_part, feat_part), 'width')  124 us
    all_gather x1, blocking collectives, local(): local_grads = lax.all_gather(cotangent, 'layer', axis=0, tiled=True)  12.6 us
  transfers between devices with their start and end apart: 3, of which 3 were waited for; matrix products, arithmetic and copies ran while one was open for 1% of the time, Pallas kernels for 0%

commit v1 on v0

--- a/solution.py
+++ b/solution.py
@@ -10,7 +10,9 @@
     local_grads = lax.all_gather(cotangent, "layer", axis=0, tiled=True)
     whole_resid, whole_grads = (
         lax.all_gather(residuals[0], "feat", axis=0, tiled=True),
-        lax.all_gather(local_grads, "feat", axis=1, tiled=True),
+        jnp.concatenate(
+            lax.all_to_all(jnp.stack([local_grads] * lax.axis_size("feat")), "feat", 0, 0), axis=1
+        ),
     )
     later_mask = (jnp.arange(layers) >= source)[:, None, None]
     used_grads = jnp.where(later_mask, whole_grads, jnp.zeros_like(whole_grads))

time: 467 us -> 375 us (0.80)
  waiting for transfers between devices: 424 us -> 312 us
  starting transfers between devices: 0.12 us -> 13.8 us
  local copies, waits for them, and re-layouts: 0.03 us -> 8.46 us
    all_gather x1 -> x0, waiting for transfers between devices: 171 us -> none  [local(): lax.all_gather(local_grads, 'feat', axis=1, tiled=True)]
    all_gather x1, waiting for transfers between devices: 127 us -> 174 us  [local(): lax.all_gather(residuals[0], 'feat', axis=0, tiled=True)]
    psum x1, waiting for transfers between devices: 124 us -> 138 us  [local(): enc_total, feat_total = lax.psum((enc_part, feat_part), 'width')]
    all_to_all x0 -> x1, starting transfers between devices: none -> 13.8 us  [local(): lax.all_to_all(jnp.stack([local_grads] * lax.axis_size('feat')), 'feat',...]
  transfers between devices with their start and end apart: 3 -> 3, of which waited for: 3 -> 2; matrix products, arithmetic and copies ran while one was open for 1% -> 1% of each run, Pallas kernels for 0% -> 0%
where the time goes in v1:
time: 375 us; the launch traced here: 374 us
  waiting for transfers between devices  312 us (83%)
  between operations  14.1 us (4%)
  starting transfers between devices  13.8 us (4%)
  matrix products  12 us (3%)
  blocking collectives  10.7 us (3%)
  local copies, waits for them, and re-layouts  8.46 us (2%)
    all_gather x1, waiting for transfers between devices, local(): lax.all_gather(residuals[0], 'feat', axis=0, tiled=True)  174 us
    psum x1, waiting for transfers between devices, local(): enc_total, feat_total = lax.psum((enc_part, feat_part), 'width')  138 us
    all_to_all x1, starting transfers between devices, local(): lax.all_to_all(jnp.stack([local_grads] * lax.axis_size('feat')), 'feat',...  13.8 us
    all_gather x1, blocking collectives, local(): local_grads = lax.all_gather(cotangent, 'layer', axis=0, tiled=True)  10.7 us
  transfers between devices with their start and end apart: 3, of which 2 were waited for; matrix products, arithmetic and copies ran while one was open for 1% of the time, Pallas kernels for 0%

profile of v1, /device:TPU:1, one launch (start us, length us, event | category | flops | bytes accessed | tf_op | source)
XLA Modules:
  0.0 374.4 jit_solution(15078776934404905618)
XLA Ops:
  7.2 0.0 copy-start
  7.2 10.7 %all_gather.6 = bf16[4,32,576]{2,1,0:T(8,128)(2,1)S(1)} all-gather(bf16[1,32,576]{2,1,0:T(8,128)(2,1)} %param.7), channel_id=1, replica_groups=mesh['layer'=4,'feat'=32,'width'=4] {'layer'}, dimensions={0}, use_global_device_ids=true | all-gather | bytes 184320 | tf_op jit(solution)/shard_map/all_gather | solution.py:10
  17.9 3.1 stack.2
  20.9 13.8 %all-to-all-start = ((bf16[32,4,32,576]{3,2,1,0:T(8,128)(2,1)}), bf16[32,4,32,576]{3,2,1,0:T(8,128)(2,1)}, u32[]{:S(2)}, u32[]{:S(2)}) async-start(bf16[32,4,32,576]{3,2,1,0:T(8,128)(2,1)} %stack.2), calls=%async_computation | async-start | bytes 10485760 | tf_op jit(solution)/shard_map/all_to_all | solution.py:14
  34.7 0.0 all-gather.3.cloned.1.call-start
  34.7 0.7 all-gather.3.cloned.1.call-update
  35.4 0.0 all-reduce.3.cloned.1.call-start
  35.5 173.7 %all-gather.3.cloned.1.call-done = bf16[1,1024,576]{2,1,0:T(8,128)(2,1)} async-done(((bf16[1,32,576]{2,1,0:T(8,128)(2,1)}), bf16[1,1024,576]{2,1,0:T(8,128)(2,1)}) %all-gather.3.cloned.1.call-update) | async-done | bytes 1179664 | tf_op jit(solution)/shard_map/all_gather | solution.py:12
  209.1 0.0 copy-done.5
  209.1 2.9 fusion.3
  212.0 0.0 all-to-all-done
  212.0 3.1 copy.13
  215.1 0.9 bitcast_select_fusion
  216.0 0.0 copy-start.1
  216.0 2.3 copy-done.1
  218.3 0.0 copy-done
  218.3 2.4 convolution_bitcast_fusion
  220.7 0.0 all-reduce.3.cloned.1.call-update
  220.8 138.0 %all-reduce.3.cloned.1.call-done = (f32[1024,256]{1,0:T(8,128)}, f32[1024,256]{1,0:T(8,128)}) async-done(((f32[1024,256]{1,0:T(8,128)}, f32[1024,256]{1,0:T(8,128)}), (f32[1024,256]{1,0:T(8,128)}, f32[1024,256]{1,0:T(8,128)})) %all-reduce.3.cloned.1.call-update) | async-done | bytes 2097168 | tf_op jit(solution)/shard_map/psum | solution.py:23
  358.8 0.0 copy-done.4
  358.8 2.1 convert_reduce_fusion
  360.9 0.0 copy-done.7
  360.9 5.3 %fusion = bf16[1,4,256,576]{2,3,1,0:T(8,128)(2,1)} fusion(bf16[4,1024,576]{2,1,0:T(8,128)(2,1)} %copy-done.1, s32[1,1024,256]{2,1,0:T(8,128)S(1)} %copy-done.4, f32[1024,256]{1,0:T(8,128)S(1)} %copy-done.6, f32[256]{0:T(256)S(1)} %bitcast.50), kind=kOutput, calls=%fused_computation.2 | convolution fusion | flops 1209597952 | bytes 7996416 | tf_op jit(solution)/shard_map/tf,ktd->kfd/dot_general | solution.py:27
  366.2 1.4 fusion.9
  (10 shorter events, 0.0 us)
Async XLA Ops:
  7.2 211.1 %copy-start = (bf16[1,4,256,576]{2,3,1,0:T(8,128)(2,1)S(1)}, bf16[1,4,256,576]{2,3,1,0:T(8,128)(2,1)}, u32[]{:S(2)}) copy-start(bf16[1,4,256,576]{2,3,1,0:T(8,128)(2,1)} %param.10) | copy-start | bytes 3538948
  20.9 188.2 %copy-start.5 = (bf16[1,576,256]{2,1,0:T(8,128)(2,1)S(1)}, bf16[1,576,256]{2,1,0:T(8,128)(2,1)}, u32[]{:S(2)}) copy-start(bf16[1,576,256]{2,1,0:T(8,128)(2,1)} %param.8) | copy-start | bytes 884740
  20.9 191.1 %all-to-all-start = ((bf16[32,4,32,576]{3,2,1,0:T(8,128)(2,1)}), bf16[32,4,32,576]{3,2,1,0:T(8,128)(2,1)}, u32[]{:S(2)}, u32[]{:S(2)}) async-start(bf16[32,4,32,576]{3,2,1,0:T(8,128)(2,1)} %stack.2), calls=%async_computation | async-start | bytes 10485760 | tf_op jit(solution)/shard_map/all_to_all | solution.py:14
  34.7 174.5 %all-gather.3.cloned.1.call-start = ((), (), s32[]{:S(2)}) async-start(), calls=%async_computation.1 | async-start | bytes 1351680 | tf_op jit(solution)/shard_map/all_gather | solution.py:12
  35.4 323.4 %all-reduce.3.cloned.1.call-start = ((), (), s32[]{:S(2)}) async-start(), calls=%async_computation.2 | async-start | bytes 4194304 | tf_op jit(solution)/shard_map/psum | solution.py:23
  216.0 2.3 copy-start.1
  220.7 138.1 %copy-start.4 = (s32[1,1024,256]{2,1,0:T(8,128)S(1)}, s32[1,1024,256]{2,1,0:T(8,128)}, u32[]{:S(2)}) copy-start(s32[1,1024,256]{2,1,0:T(8,128)} %param.11) | copy-start | bytes 3145732
  220.7 140.2 %copy-start.7 = (f32[1,256]{1,0:T(1,128)S(1)}, f32[1,256]{1,0:T(1,128)}, u32[]{:S(2)}) copy-start(f32[1,256]{1,0:T(1,128)} %param.9) | copy-start | bytes 3076
  358.8 2.1 copy-start.6
  360.9 5.4 %copy-start.3 = (bf16[1024,256]{1,0:T(8,128)(2,1)}, bf16[1024,256]{1,0:T(8,128)(2,1)S(1)}, u32[]{:S(2)}) copy-start(bf16[1024,256]{1,0:T(8,128)(2,1)S(1)} %get-tuple-element.7) | copy-start | bytes 1572868
  360.9 5.4 %copy-start.2 = (bf16[1,1024,576]{2,1,0:T(8,128)(2,1)S(1)}, bf16[1,1024,576]{2,1,0:T(8,128)(2,1)}, u32[]{:S(2)}) copy-start(bf16[1,1024,576]{2,1,0:T(8,128)(2,1)} %all-gather.3.cloned.1.call-done) | copy-start | bytes 3538948
Sparse Core Ops, SparseCore 0:
  37.6 171.5 all-gather.2
  220.9 137.8 all-reduce.2
